TPU v7x, 128 devices: a whole 4x4x4 slice. The times are simulated.
128 devices in a mesh: dp: 8 (over x, core), adapter: 16 (over z, y).
Axes of the slice: x: 4, y: 4, z: 4, core: 2. Of those that a mesh axis runs over, the one named last changes fastest.
Arguments:
- residual_input: bfloat16 [65536, 2560], P(('dp', 'adapter')), may hold values from -6 to 6
- input_norm_gain: float32 [2560], replicated, may hold values from 0.5 to 1.5
- base_projection_weight: bfloat16 [2560, 4096], P('adapter', 'dp'), may hold values from -0.125 to 0.125
- query_key_gains: float32 [2, 256], replicated, may hold values from 0.5 to 1.5
- adapter_down_weight: bfloat16 [64, 2560, 48], P('adapter'), may hold values from -0.125 to 0.125
- adapter_up_weight: bfloat16 [64, 16, 4096], P('adapter'), may hold values from -1.5 to 1.5
- row_adapter_index: int32 [65536, 1], P(('dp', 'adapter')), may hold values from 0 to 63; in each aligned block of 512 rows (0 to 511, 512 to 1023, ...) at most 16 rows name the same one
- row_sequence_index: int32 [65536], P(('dp', 'adapter')), may hold values from 0 to 7, never falling along the last dimension, each value on 1 to 12288 neighbouring positions
Outputs:
- attended: bfloat16 [65536, 2048], P(('dp', 'adapter'))
Inputs may be any that keep to these rules, and one draw needn't show every extreme that they name: `row_adapter_index`: among the rows of one device, no adapter serves more than 16 rows; some adapter serves exactly 16 rows of some device. `row_sequence_index`: sequence numbers never fall along the rows; every sequence has 1 to 12288 rows, one exactly 12288.
All inputs are finite; a program needn't handle non-finite values.
Results may differ from a plain program's by a relative error of at most 0.02.
Values may be sent and summed in bfloat16 or wider, within the bound.
A program may use at most 128 MiB of HBM per device.

v0:
```python
import jax
import jax.numpy as jnp
from jax import lax
from jax.sharding import PartitionSpec as P

HEADS = 8
KV_HEADS = 4
HEAD_DIM = 256
WINDOW = 1024


def shifted(value, axis, by):
    size = lax.axis_size(axis)
    pairs = [(i, i + by) for i in range(size) if 0 <= i + by < size]
    return lax.ppermute(value, axis, pairs)


def head_norm(block, heads, gain):
    shaped = block.reshape(block.shape[0], heads, HEAD_DIM)
    scaled = shaped * lax.rsqrt(jnp.mean(shaped * shaped, axis=-1, keepdims=True) + 1e-06) * gain
    return scaled.astype(jnp.bfloat16)


def adapter_delta(rank_values, up_matrices):
    width_q = HEADS * HEAD_DIM
    width_k = KV_HEADS * HEAD_DIM
    inner = up_matrices.shape[1]
    part_q = jnp.einsum(
        "nacr,arq->nacq",
        rank_values[..., 0:inner],
        up_matrices[:, :, 0:width_q],
        preferred_element_type=jnp.float32,
    )
    part_k = jnp.einsum(
        "nacr,arq->nacq",
        rank_values[..., inner : 2 * inner],
        up_matrices[:, :, width_q : width_q + width_k],
        preferred_element_type=jnp.float32,
    )
    part_v = jnp.einsum(
        "nacr,arq->nacq",
        rank_values[..., 2 * inner : 3 * inner],
        up_matrices[:, :, width_q + width_k :],
        preferred_element_type=jnp.float32,
    )
    return jnp.concatenate([part_q, part_k, part_v], axis=-1).astype(jnp.bfloat16)


def adapter_ranks(adapter_slots, down_matrices):
    return jnp.einsum(
        "nacd,adr->nacr", adapter_slots, down_matrices, preferred_element_type=jnp.float32
    ).astype(jnp.bfloat16)


def body(
    residual_input,
    input_norm_gain,
    base_projection_weight,
    query_key_gains,
    adapter_down_weight,
    adapter_up_weight,
    row_adapter_index,
    row_sequence_index,
):
    rows = residual_input.shape[0]
    width = residual_input.shape[1]
    width_q = HEADS * HEAD_DIM
    width_k = KV_HEADS * HEAD_DIM
    group = HEADS // KV_HEADS
    values_in = residual_input.astype(jnp.float32)
    normed = (
        values_in
        * lax.rsqrt(jnp.mean(values_in * values_in, axis=-1, keepdims=True) + 1e-06)
        * input_norm_gain
    ).astype(jnp.bfloat16)
    slab = lax.all_gather(base_projection_weight, "dp", axis=1, tiled=True)
    base = jnp.dot(
        normed,
        lax.all_gather(slab, "adapter", axis=0, tiled=True),
        preferred_element_type=jnp.float32,
    ).astype(jnp.bfloat16)
    total_width = base.shape[1]
    owners = lax.axis_size("adapter")
    local_adapter_count = adapter_down_weight.shape[0]
    adapters_all = owners * local_adapter_count
    capacity = 2 * rows // adapters_all
    adapter_ids = row_adapter_index[:, 0]
    onehot = (adapter_ids[:, None] == jnp.arange(adapters_all, dtype=jnp.int32)[None, :]).astype(
        jnp.int32
    )
    earlier = jnp.cumsum(onehot, axis=0) - onehot
    place = jnp.sum(earlier * onehot, axis=1)
    slot = adapter_ids * capacity + place
    scratch_buffer = jnp.zeros((adapters_all * capacity, width), jnp.bfloat16).at[slot].set(normed)
    scratch_buffer = scratch_buffer.reshape(owners, local_adapter_count, capacity, width)
    adapter_corrections = adapter_delta(
        adapter_ranks(
            lax.all_to_all(scratch_buffer, "adapter", split_axis=0, concat_axis=0, tiled=True),
            adapter_down_weight,
        ),
        adapter_up_weight,
    )
    returned = lax.all_to_all(
        adapter_corrections, "adapter", split_axis=0, concat_axis=0, tiled=True
    )
    delta_slots = returned.reshape(adapters_all * capacity, total_width)
    delta_update = delta_slots[slot]
    projected = base.astype(jnp.float32) + delta_update.astype(jnp.float32)
    queries = head_norm(projected[:, 0:width_q], HEADS, query_key_gains[0]).reshape(
        rows, KV_HEADS, group, HEAD_DIM
    )
    keys = head_norm(
        projected[:, width_q : width_q + width_k], KV_HEADS, query_key_gains[1]
    ).reshape(rows, width_k)
    values = projected[:, width_q + width_k :].astype(jnp.bfloat16)
    before = (WINDOW + rows - 2) // rows
    key_parts = []
    value_parts = []
    seg_parts = []
    for offset in range(before, 0, -1):
        moved_keys, moved_values, moved_seg = shifted(
            (keys, values, row_sequence_index), ("dp", "adapter"), offset
        )
        key_parts.append(moved_keys)
        value_parts.append(moved_values)
        seg_parts.append(moved_seg)
    key_parts.append(keys)
    value_parts.append(values)
    seg_parts.append(row_sequence_index)
    span = (before + 1) * rows
    key_all = jnp.concatenate(key_parts, axis=0).reshape(span, KV_HEADS, HEAD_DIM)
    value_all = jnp.concatenate(value_parts, axis=0).reshape(span, KV_HEADS, HEAD_DIM)
    seg_all = jnp.concatenate(seg_parts, axis=0)
    position = lax.axis_index(("dp", "adapter"))
    query_pos = position * rows + jnp.arange(rows, dtype=jnp.int32)
    key_pos = (position - before) * rows + jnp.arange(span, dtype=jnp.int32)
    gap = query_pos[:, None] - key_pos[None, :]
    allowed = (
        (row_sequence_index[:, None] == seg_all[None, :])
        & (gap >= 0)
        & (gap < WINDOW)
        & (key_pos[None, :] >= 0)
    )
    scores = jnp.einsum(
        "tkgd,skd->kgts", queries, key_all, preferred_element_type=jnp.float32
    ) * HEAD_DIM ** (-0.5)
    weights = jnp.where(allowed[None, None], jnp.exp(scores), jnp.float32(0.0))
    total = jnp.sum(weights, axis=-1)
    probs = weights.astype(jnp.bfloat16)
    summed = jnp.einsum("kgts,skd->tkgd", probs, value_all, preferred_element_type=jnp.float32)
    result = summed / jnp.transpose(total, (2, 0, 1))[..., None]
    return result.reshape(rows, width_q).astype(jnp.bfloat16)


def solution(mesh):
    placed = (
        P(("dp", "adapter"), None),
        P(),
        P("adapter", "dp"),
        P(),
        P("adapter", None, None),
        P("adapter", None, None),
        P(("dp", "adapter"), None),
        P(("dp", "adapter")),
    )
    return jax.shard_map(
        body, mesh=mesh, in_specs=placed, out_specs=P(("dp", "adapter"), None), check_vma=False
    )
```

profile of v0, /device:TPU:3, one launch (start us, length us, event | category | flops | bytes accessed | tf_op | source)
XLA Modules:
  0.0 495.9 jit_solution(7275896673530061145)
XLA Ops:
  7.3 26.8 %all-gather.3.cloned.1.call-done = bf16[160,4096]{1,0:T(8,128)(2,1)} async-done(((bf16[160,512]{1,0:T(8,128)(2,1)}), bf16[160,4096]{1,0:T(8,128)(2,1)}) %all-gather.3.cloned.1.call-update) | async-done | bytes 1310736 | tf_op jit(solution)/shard_map/all_gather | solution.py:76
  37.2 2.3 fusion.7
  39.5 9.0 %scatter_custom_fusion = bf16[1024,2560]{1,0:T(8,128)(2,1)} fusion(s32[512]{0:T(512)S(1)} %bitcast.120, bf16[]{:T(256)} %constant.17.clone.1, bf16[512,2560]{1,0:T(8,128)(2,1)} %param.8, f32[2560]{0:T(1024)S(1)} %copy-done.8, f32[512]{0:T(512)S(1)} %add_rsqrt_fusion.2), kind=kCustom, calls=%fused_computation.37 | custom fusion | flops 5242880 | bytes 7878658 | tf_op jit(solution)/shard_map/scatter | solution.py:94
  48.5 83.8 %all_to_all.10 = bf16[16,4,16,2560]{3,2,1,0:T(8,128)(2,1)S(1)} all-to-all(bf16[16,4,16,2560]{3,2,1,0:T(8,128)(2,1)} %bitcast.105), channel_id=1, replica_groups=mesh['dp'=8,'adapter'=16] {'adapter'}, dimensions={0} | all-to-all | bytes 10485760 | tf_op jit(solution)/shard_map/all_to_all | solution.py:98
  136.6 4.3 pad_maximum_fusion
  140.9 8.3 %copy.62 = bf16[16,4,16,4096]{3,2,1,0:T(8,128)(2,1)} copy(bf16[16,4,16,4096]{3,2,0,1:T(8,128)(2,1)} %pad_maximum_fusion) | data formatting | bytes 16777216 | tf_op jit(solution)/shard_map/concatenate | solution.py:46
  149.2 5.1 %all-to-all-start.1 = ((bf16[16,4,16,4096]{3,2,1,0:T(8,128)(2,1)}), bf16[16,4,16,4096]{3,2,1,0:T(8,128)(2,1)}, u32[]{:S(2)}, u32[]{:S(2)}) async-start(bf16[16,4,16,4096]{3,2,1,0:T(8,128)(2,1)} %copy.62), calls=%async_computation.1 | async-start | bytes 16777216 | tf_op jit(solution)/shard_map/all_to_all | solution.py:103
  154.3 3.1 collective-permute-start.3
  157.4 4.3 collective-permute-start.2
  161.8 151.0 %collective-permute-done.3 = s32[512]{0:T(512)S(1)} collective-permute-done((s32[512]{0:T(512)S(1)}, s32[512]{0:T(512)S(1)}, u32[]{:S(2)}, u32[]{:S(2)}) %collective-permute-start.3) | collective-permute-done | bytes 2080 | tf_op jit(solution)/shard_map/ppermute | solution.py:15
  312.8 15.8 %collective-permute-done.2 = s32[512]{0:T(512)S(1)} collective-permute-done((s32[512]{0:T(512)S(1)}, s32[512]{0:T(512)S(1)}, u32[]{:S(2)}, u32[]{:S(2)}) %collective-permute-start.2) | collective-permute-done | bytes 2080 | tf_op jit(solution)/shard_map/ppermute | solution.py:15
  328.6 2.5 fusion.22
  331.1 13.0 %gather_fusion = bf16[512,4096]{1,0:T(8,128)(2,1)} fusion(bf16[1024,4096]{1,0:T(8,128)(2,1)} %bitcast.18, s32[1024]{0:T(1024)S(1)} %pad_clamp_fusion), kind=kCustom, calls=%fused_computation | custom fusion | bytes 8390656 | tf_op jit(solution)/shard_map/gather | solution.py:107
  344.1 16.6 %convert_add_fusion = f32[512,4096]{1,0:T(8,128)S(1)} fusion(bf16[512,4096]{1,0:T(8,128)(2,1)} %gather_fusion, bf16[2560,4096]{1,0:T(8,128)(2,1)} %all-gather.5.cloned.1.call-done, bf16[512,2560]{1,0:T(8,128)(2,1)} %param.8, f32[2560]{0:T(1024)S(1)} %copy-done.8, f32[512]{0:T(512)S(1)} %add_rsqrt_fusion.2), kind=kOutput, calls=%fused_computation.10 | convolution fusion | flops 10751049728 | bytes 36188160 | tf_op jit(solution)/shard_map/dot_general | solution.py:77
  362.0 1.9 collective-permute-start.1
  363.9 1.9 collective-permute-start
  367.4 2.2 mul.115
  371.3 2.3 multiply_convert_fusion
  373.6 2.1 collective-permute-start.5
  375.7 3.1 collective-permute-start.4
  378.9 4.3 slice_multiply_fusion.1
  383.2 6.6 %reshape.168 = f32[512,4,2,256]{3,2,1,0:T(2,128)} reshape(f32[512,2048]{1,0:T(8,128)} %get-tuple-element.6) | data formatting | bytes 8388608 | tf_op jit(solution)/shard_map/reshape | solution.py:19
  389.8 6.1 %copy.87 = f32[64,8,8,256]{3,2,1,0:T(8,128)} copy(f32[64,8,8,256]{3,1,2,0:T(8,128)} %bitcast.106) | data formatting | bytes 8388608
  395.9 2.8 reduce_sum.51
  399.9 36.2 %collective-permute-done.1 = bf16[512,1024]{1,0:T(8,128)(2,1)} collective-permute-done((bf16[512,1024]{1,0:T(8,128)(2,1)}, bf16[512,1024]{1,0:T(8,128)(2,1)}, u32[]{:S(2)}, u32[]{:S(2)}) %collective-permute-start.1) | collective-permute-done | bytes 1048608 | tf_op jit(solution)/shard_map/ppermute | solution.py:15
  436.1 3.2 pad_maximum_fusion.1
  439.3 4.8 copy.80
  444.0 14.5 %collective-permute-done.5 = bf16[512,1024]{1,0:T(8,128)(2,1)} collective-permute-done((bf16[512,1024]{1,0:T(8,128)(2,1)S(1)}, bf16[512,1024]{1,0:T(8,128)(2,1)}, u32[]{:S(2)}, u32[]{:S(2)}) %collective-permute-start.5) | collective-permute-done | bytes 1048608 | tf_op jit(solution)/shard_map/ppermute | solution.py:15
  458.5 2.3 copy.108
  462.1 13.2 %fusion = (f32[4,2,512]{2,1,0:T(2,128)S(1)}, f32[4,1536,512,2]{2,1,3,0:T(8,128)}) fusion(pred[512,1536]{0,1:T(8,128)(4,1)S(1)} %copy-done.5, f32[512,4,2,256]{3,2,1,0:T(2,128)S(1)} %copy-done.4, f32[256]{0:T(256)S(1)} %bitcast.123, f32[512,4,2]{0,2,1:T(2,128)S(1)} %rsqrt.30, bf16[512,4,256]{2,0,1:T(8,128)(2,1)} %bitcast.113, ...), kind=kOutput, calls=%fused_computation.3 | convolution fusion | flops 3252678656 | bytes 33326080 | tf_op jit(solution)/shard_map/tkgd,skd->kgts/dot_general | solution.py:144
  475.3 11.4 %fusion.12 = bf16[512,4,2,256]{0,3,2,1:T(8,128)(2,1)S(1)} fusion(bf16[1536,4,256,1]{0,2,3,1:T(8,128)(2,1)} %bitcast.111, f32[4,1536,512,2]{2,1,3,0:T(8,128)} %get-tuple-element.10, pred[512,1536]{0,1:T(8,128)(4,1)} %fusion.22, f32[512,4,2]{0,2,1:T(2,128)S(1)} %bitcast.124), kind=kOutput, calls=%fused_computation.22 | convolution fusion | flops 3242196992 | bytes 31211520 | tf_op jit(solution)/shard_map/kgts,skd->tkgd/dot_general | solution.py:150
  486.7 2.4 copy.72
  (61 shorter events, 15.0 us)
Async XLA Ops:
  6.5 125.8 %copy-start = (bf16[4,2560,48]{1,2,0:T(8,128)(2,1)S(1)}, bf16[4,2560,48]{1,2,0:T(8,128)(2,1)}, u32[]{:S(2)}) copy-start(bf16[4,2560,48]{1,2,0:T(8,128)(2,1)} %param.12) | copy-start | bytes 2949124
  6.5 33.0 %copy-start.7 = (s32[512,1]{0,1:T(1,128)S(1)}, s32[512,1]{0,1:T(1,128)}, u32[]{:S(2)}) copy-start(s32[512,1]{0,1:T(1,128)} %param.14) | copy-start | bytes 6148
  6.5 33.0 %copy-start.8 = (f32[2560]{0:T(1024)S(1)}, f32[2560]{0:T(1024)}, u32[]{:S(2)}) copy-start(f32[2560]{0:T(1024)} %param.9) | copy-start | bytes 30724
  6.5 27.6 %all-gather.3.cloned.1.call-start = ((), (), s32[]{:S(2)}) async-start(), calls=%async_computation.2 | async-start | bytes 1474560 | tf_op jit(solution)/shard_map/all_gather | solution.py:76
  7.3 336.8 %all-gather.5.cloned.1.call-start = ((), (), s32[]{:S(2)}) async-start(), calls=%async_computation.3 | async-start | bytes 22282240 | tf_op jit(solution)/shard_map/all_gather | solution.py:79
  132.4 1.5 copy-start.6
  149.2 5.1 %copy-start.9 = (s32[512]{0:T(512)S(1)}, s32[512]{0:T(512)}, u32[]{:S(2)}) copy-start(s32[512]{0:T(512)} %param.15) | copy-start | bytes 6148
  149.2 12.6 %copy-start.10 = (f32[2,256]{1,0:T(2,128)S(1)}, f32[2,256]{1,0:T(2,128)}, u32[]{:S(2)}) copy-start(f32[2,256]{1,0:T(2,128)} %param.11) | copy-start | bytes 6148
  149.2 181.9 %all-to-all-start.1 = ((bf16[16,4,16,4096]{3,2,1,0:T(8,128)(2,1)}), bf16[16,4,16,4096]{3,2,1,0:T(8,128)(2,1)}, u32[]{:S(2)}, u32[]{:S(2)}) async-start(bf16[16,4,16,4096]{3,2,1,0:T(8,128)(2,1)} %copy.62), calls=%async_computation.1 | async-start | bytes 16777216 | tf_op jit(solution)/shard_map/all_to_all | solution.py:103
  154.3 158.5 %collective-permute-start.3 = (s32[512]{0:T(512)S(1)}, s32[512]{0:T(512)S(1)}, u32[]{:S(2)}, u32[]{:S(2)}) collective-permute-start(s32[512]{0:T(512)S(1)} %copy-done.9), channel_id=1, source_target_pairs={{0,1},{1,2},{2,3},{3,4},{4,5},{5,6},{6,7},{7,8},{8,9},{9,10},{10,1... | collective-permute-start | bytes 6152 | tf_op jit(solution)/shard_map/ppermute | solution.py:15
  157.4 171.2 %collective-permute-start.2 = (s32[512]{0:T(512)S(1)}, s32[512]{0:T(512)S(1)}, u32[]{:S(2)}, u32[]{:S(2)}) collective-permute-start(s32[512]{0:T(512)S(1)} %copy-done.9), channel_id=1, source_target_pairs={{0,2},{1,3},{2,4},{3,5},{4,6},{5,7},{6,8},{7,9},{8,10},{9,11},{10,... | collective-permute-start | bytes 6152 | tf_op jit(solution)/shard_map/ppermute | solution.py:15
  360.7 5.1 %copy-start.2 = (f32[512,4096]{1,0:T(8,128)}, f32[512,4096]{1,0:T(8,128)S(1)}, u32[]{:S(2)}) copy-start(f32[512,4096]{1,0:T(8,128)S(1)} %convert_add_fusion) | copy-start | bytes 25165828
  362.0 74.0 %collective-permute-start.1 = (bf16[512,1024]{1,0:T(8,128)(2,1)}, bf16[512,1024]{1,0:T(8,128)(2,1)}, u32[]{:S(2)}, u32[]{:S(2)}) collective-permute-start(bf16[512,1024]{1,0:T(8,128)(2,1)} %slice.85), channel_id=1, source_target_pairs={{0,1},{1,2},{2,3},{3,4},{4,5},{5,6},{6,7},{7,8},{8,9},{9,10},{10,1... | collective-permute-start | bytes 3145736 | tf_op jit(solution)/shard_map/ppermute | solution.py:15
  363.9 72.1 %collective-permute-start = (bf16[512,1024]{1,0:T(8,128)(2,1)}, bf16[512,1024]{1,0:T(8,128)(2,1)}, u32[]{:S(2)}, u32[]{:S(2)}) collective-permute-start(bf16[512,1024]{1,0:T(8,128)(2,1)} %slice.85), channel_id=1, source_target_pairs={{0,2},{1,3},{2,4},{3,5},{4,6},{5,7},{6,8},{7,9},{8,10},{9,11},{10,... | collective-permute-start | bytes 3145736 | tf_op jit(solution)/shard_map/ppermute | solution.py:15
  370.9 8.0 %copy-start.3 = (f32[512,4096]{1,0:T(8,128)S(1)}, f32[512,4096]{1,0:T(8,128)}, u32[]{:S(2)}) copy-start(f32[512,4096]{1,0:T(8,128)} %copy-done.2) | copy-start | bytes 25165828
  373.6 84.9 %collective-permute-start.5 = (bf16[512,1024]{1,0:T(8,128)(2,1)S(1)}, bf16[512,1024]{1,0:T(8,128)(2,1)}, u32[]{:S(2)}, u32[]{:S(2)}) collective-permute-start(bf16[512,1024]{1,0:T(8,128)(2,1)S(1)} %multiply_convert_fusion), channel_id=1, source_target_pairs={{0,1},{1,2},{2,3},{3,4},{4,5},{5,6},{6,7},{7,8},{8,9},{9,10},{10,1... | collective-permute-start | bytes 3145736 | tf_op jit(solution)/shard_map/ppermute | solution.py:15
  375.7 85.1 %collective-permute-start.4 = (bf16[512,1024]{1,0:T(8,128)(2,1)S(1)}, bf16[512,1024]{1,0:T(8,128)(2,1)}, u32[]{:S(2)}, u32[]{:S(2)}) collective-permute-start(bf16[512,1024]{1,0:T(8,128)(2,1)S(1)} %multiply_convert_fusion), channel_id=1, source_target_pairs={{0,2},{1,3},{2,4},{3,5},{4,6},{5,7},{6,8},{7,9},{8,10},{9,11},{10,... | collective-permute-start | bytes 3145736 | tf_op jit(solution)/shard_map/ppermute | solution.py:15
  439.3 22.8 %copy-start.5 = (pred[512,1536]{0,1:T(8,128)(4,1)S(1)}, pred[512,1536]{0,1:T(8,128)(4,1)}, u32[]{:S(2)}) copy-start(pred[512,1536]{0,1:T(8,128)(4,1)} %fusion.22) | copy-start | bytes 2359300
  444.0 18.1 %copy-start.4 = (f32[512,4,2,256]{3,2,1,0:T(2,128)S(1)}, f32[512,4,2,256]{3,2,1,0:T(2,128)}, u32[]{:S(2)}) copy-start(f32[512,4,2,256]{3,2,1,0:T(2,128)} %reshape.168) | copy-start | bytes 12582916
  475.3 13.8 %copy-start.1 = (bf16[4,2560,48]{1,2,0:T(8,128)(2,1)S(1)}, bf16[4,2560,48]{1,2,0:T(8,128)(2,1)}, u32[]{:S(2)}) copy-start(bf16[4,2560,48]{1,2,0:T(8,128)(2,1)} %param.12) | copy-start | bytes 2949124
Sparse Core Ops, SparseCore 0:
  9.1 25.0 all-gather.2
  36.3 278.7 all-gather.4
where the time goes:
time: 497 us; the launch traced here: 496 us
  waiting for transfers between devices  245 us (49%)
  blocking collectives  83.8 us (17%)
  local copies, waits for them, and re-layouts  50.7 us (10%)
  matrix products  45.4 us (9%)
  other arithmetic  35.7 us (7%)
  starting transfers between devices  21.5 us (4%)
  between operations  13.8 us (3%)
    ppermute x6, waiting for transfers between devices, shifted(): return lax.ppermute(value, axis, pairs)  217 us
    all_to_all x1, blocking collectives, body(): lax.all_to_all(scratch_buffer, 'adapter', split_axis=0, concat_axis=0, ti...  83.8 us
    all_gather x1, waiting for transfers between devices, body(): slab = lax.all_gather(base_projection_weight, 'dp', axis=1, tiled=True)  26.8 us
    dot_general x1, matrix products, body(): jnp.dot(normed, lax.all_gather(slab, 'adapter', axis=0, tiled=True), pref...  16.6 us
    ppermute x6, starting transfers between devices, shifted(): return lax.ppermute(value, axis, pairs)  16.4 us
    dot_general x1, matrix products, body(): jnp.einsum('tkgd,skd->kgts', queries, key_all, preferred_element_type=jnp...  13.2 us
    gather x1, local copies, waits for them, and re-layouts, body(): delta_update = delta_slots[slot]  13 us
    dot_general x1, matrix products, body(): jnp.einsum('kgts,skd->tkgd', probs, value_all, preferred_element_type=jnp...  11.4 us
  transfers between devices with their start and end apart: 9, of which 5 were waited for; matrix products, arithmetic and copies ran while one was open for 17% of the time, Pallas kernels for 0%

commit v1 on v0

--- a/solution.py
+++ b/solution.py
@@ -2,11 +2,15 @@
 import jax.numpy as jnp
 from jax import lax
 from jax.sharding import PartitionSpec as P
+from jax.lax import all_to_all, psum
 
 HEADS = 8
 KV_HEADS = 4
 HEAD_DIM = 256
 WINDOW = 1024
+list_rings = lambda message, which_axis: jnp.concatenate(
+    all_to_all(jnp.stack(psum(1, which_axis) * [message]), which_axis, 0, 0), axis=0
+)
 
 
 def shifted(value, axis, by):
@@ -74,11 +78,9 @@
         * input_norm_gain
     ).astype(jnp.bfloat16)
     slab = lax.all_gather(base_projection_weight, "dp", axis=1, tiled=True)
-    base = jnp.dot(
-        normed,
-        lax.all_gather(slab, "adapter", axis=0, tiled=True),
-        preferred_element_type=jnp.float32,
-    ).astype(jnp.bfloat16)
+    base = jnp.dot(normed, list_rings(slab, "adapter"), preferred_element_type=jnp.float32).astype(
+        jnp.bfloat16
+    )
     total_width = base.shape[1]
     owners = lax.axis_size("adapter")
     local_adapter_count = adapter_down_weight.shape[0]

time: 497 us -> 729 us (1.47)
  waiting for transfers between devices: 245 us -> 477 us
  blocking collectives: 83.8 us -> 68.8 us
  local copies, waits for them, and re-layouts: 50.7 us -> 59.6 us
    ppermute x6, waiting for transfers between devices: 217 us -> 356 us  [shifted(): return lax.ppermute(value, axis, pairs)]
    all_to_all x1, waiting for transfers between devices: 0.01 us -> 93 us  [body(): lax.all_to_all(adapter_corrections, 'adapter', split_axis=0, concat_axis=...]
    all_to_all x1, blocking collectives: 83.8 us -> 68.8 us  [body(): lax.all_to_all(scratch_buffer, 'adapter', split_axis=0, concat_axis=0, ti...]
    another operation x1 -> x2, local copies, waits for them, and re-layouts: 0.01 us -> 8.36 us  [the longest x1 8.35 us: jnp.stack(psum(1, which_axis) * [message])]
  transfers between devices with their start and end apart: 9 -> 9, of which waited for: 5 -> 7; matrix products, arithmetic and copies ran while one was open for 17% -> 5% of each run, Pallas kernels for 0% -> 0%
where the time goes in v1:
time: 729 us; the launch traced here: 726 us
  waiting for transfers between devices  477 us (65%)
  blocking collectives  68.8 us (9%)
  local copies, waits for them, and re-layouts  59.6 us (8%)
  matrix products  45.4 us (6%)
  other arithmetic  34 us (5%)
  starting transfers between devices  27.4 us (4%)
  between operations  13.7 us (2%)
    ppermute x6, waiting for transfers between devices, shifted(): return lax.ppermute(value, axis, pairs)  356 us
    all_to_all x1, waiting for transfers between devices, body(): lax.all_to_all(adapter_corrections, 'adapter', split_axis=0, concat_axis=...  93 us
    all_to_all x1, blocking collectives, body(): lax.all_to_all(scratch_buffer, 'adapter', split_axis=0, concat_axis=0, ti...  68.8 us
    all_gather x1, waiting for transfers between devices, body(): slab = lax.all_gather(base_projection_weight, 'dp', axis=1, tiled=True)  27.3 us
    ppermute x6, starting transfers between devices, shifted(): return lax.ppermute(value, axis, pairs)  17 us
    dot_general x1, matrix products, body(): jnp.dot(normed, list_rings(slab, 'adapter'), preferred_element_type=jnp.f...  16.8 us
  transfers between devices with their start and end apart: 9, of which 7 were waited for; matrix products, arithmetic and copies ran while one was open for 5% of the time, Pallas kernels for 0%

profile of v1, /device:TPU:3, one launch (start us, length us, event | category | flops | bytes accessed | tf_op | source)
XLA Modules:
  0.0 725.7 jit_solution(6210403250057828103)
XLA Ops:
  10.3 2.3 fusion.7
  12.6 8.8 %scatter_custom_fusion = bf16[1024,2560]{1,0:T(8,128)(2,1)} fusion(s32[512]{0:T(512)S(1)} %bitcast.121, bf16[]{:T(256)} %constant.17.clone.1, bf16[512,2560]{1,0:T(8,128)(2,1)} %param.8, f32[2560]{0:T(1024)} %param.9, f32[512]{0:T(512)S(1)} %add_rsqrt_fusion.2), kind=kCustom, calls=%fused_computation.37 | custom fusion | flops 5242880 | bytes 7876610 | tf_op jit(solution)/shard_map/scatter | solution.py:96
  21.4 68.8 %all_to_all.15 = bf16[16,4,16,2560]{3,2,1,0:T(8,128)(2,1)S(1)} all-to-all(bf16[16,4,16,2560]{3,2,1,0:T(8,128)(2,1)} %bitcast.106), channel_id=1, replica_groups=mesh['dp'=8,'adapter'=16] {'adapter'}, dimensions={0} | all-to-all | bytes 10485760 | tf_op jit(solution)/shard_map/all_to_all | solution.py:100
  94.5 3.7 pad_maximum_fusion
  98.2 7.7 %copy.62 = bf16[16,4,16,4096]{3,2,1,0:T(8,128)(2,1)} copy(bf16[16,4,16,4096]{3,2,0,1:T(8,128)(2,1)} %pad_maximum_fusion) | data formatting | bytes 16777216 | tf_op jit(solution)/shard_map/concatenate | solution.py:50
  106.0 4.9 all-to-all-start.2
  111.7 27.3 %all-gather.2.cloned.1.call-done = bf16[160,4096]{1,0:T(8,128)(2,1)} async-done(((bf16[160,512]{1,0:T(8,128)(2,1)}), bf16[160,4096]{1,0:T(8,128)(2,1)}) %all-gather.2.cloned.1.call-update) | async-done | bytes 1310736 | tf_op jit(solution)/shard_map/all_gather | solution.py:80
  139.0 93.0 %all-to-all-done.2 = bf16[16,4,16,4096]{3,2,1,0:T(8,128)(2,1)} async-done(((bf16[16,4,16,4096]{3,2,1,0:T(8,128)(2,1)}), bf16[16,4,16,4096]{3,2,1,0:T(8,128)(2,1)}, u32[]{:S(2)}, u32[]{:S(2)}) %all-to-all-start.2) | async-done | bytes 8388640 | tf_op jit(solution)/shard_map/all_to_all | solution.py:105
  232.0 8.4 %stack.2 = bf16[16,160,4096]{2,1,0:T(8,128)(2,1)} broadcast(bf16[160,4096]{1,0:T(8,128)(2,1)} %all-gather.2.cloned.1.call-done), dimensions={1,2} | broadcast | bytes 22282240 | tf_op jit(solution)/shard_map/stack | solution.py:12
  240.3 5.5 all-to-all-start
  245.8 4.6 collective-permute-start.2
  252.7 298.8 %collective-permute-done.2 = s32[512]{0:T(512)S(1)} collective-permute-done((s32[512]{0:T(512)S(1)}, s32[512]{0:T(512)S(1)}, u32[]{:S(2)}, u32[]{:S(2)}) %collective-permute-start.2) | collective-permute-done | bytes 2080 | tf_op jit(solution)/shard_map/ppermute | solution.py:19
  551.5 13.1 %gather_fusion = bf16[512,4096]{1,0:T(8,128)(2,1)} fusion(bf16[1024,4096]{1,0:T(8,128)(2,1)} %bitcast.19, s32[1024]{0:T(1024)S(1)} %pad_clamp_fusion), kind=kCustom, calls=%fused_computation | custom fusion | bytes 8390656 | tf_op jit(solution)/shard_map/gather | solution.py:109
  564.7 16.8 %convert_add_fusion = f32[512,4096]{1,0:T(8,128)S(1)} fusion(bf16[512,4096]{1,0:T(8,128)(2,1)} %gather_fusion, bf16[2560,4096]{1,0:T(8,128)(2,1)} %bitcast, bf16[512,2560]{1,0:T(8,128)(2,1)} %param.8, f32[2560]{0:T(1024)S(1)} %copy-done.9, f32[512]{0:T(512)S(1)} %add_rsqrt_fusion.2), kind=kOutput, calls=%fused_computation.10 | convolution fusion | flops 10751049728 | bytes 36188160 | tf_op jit(solution)/shard_map/dot_general | solution.py:81
  581.5 3.2 copy-done.2
  594.5 2.8 collective-permute-start.4
  597.5 2.9 collective-permute-start
  600.4 2.4 collective-permute-start.1
  602.8 2.5 fusion.22
  606.4 2.7 slice_multiply_fusion.1
  609.1 3.9 copy.87
  613.0 2.8 reduce_sum.51
  616.0 6.6 reshape.174
  622.5 32.2 %collective-permute-done.5 = bf16[512,1024]{1,0:T(8,128)(2,1)} collective-permute-done((bf16[512,1024]{1,0:T(8,128)(2,1)S(1)}, bf16[512,1024]{1,0:T(8,128)(2,1)}, u32[]{:S(2)}, u32[]{:S(2)}) %collective-permute-start.5) | collective-permute-done | bytes 1048608 | tf_op jit(solution)/shard_map/ppermute | solution.py:19
  657.0 4.5 collective-permute-done.4
  663.9 8.9 %collective-permute-done = bf16[512,1024]{1,0:T(8,128)(2,1)} collective-permute-done((bf16[512,1024]{1,0:T(8,128)(2,1)S(1)}, bf16[512,1024]{1,0:T(8,128)(2,1)}, u32[]{:S(2)}, u32[]{:S(2)}) %collective-permute-start) | collective-permute-done | bytes 1048608 | tf_op jit(solution)/shard_map/ppermute | solution.py:19
  672.8 11.3 %collective-permute-done.1 = bf16[512,1024]{1,0:T(8,128)(2,1)} collective-permute-done((bf16[512,1024]{1,0:T(8,128)(2,1)S(1)}, bf16[512,1024]{1,0:T(8,128)(2,1)}, u32[]{:S(2)}, u32[]{:S(2)}) %collective-permute-start.1) | collective-permute-done | bytes 1048608 | tf_op jit(solution)/shard_map/ppermute | solution.py:19
  684.1 3.0 pad_maximum_fusion.1
  687.1 4.9 copy.80
  692.0 13.9 %fusion = (f32[4,2,512]{2,1,0:T(2,128)S(1)}, f32[4,1536,512,2]{2,1,3,0:T(8,128)}) fusion(pred[512,1536]{0,1:T(8,128)(4,1)S(1)} %copy-done.7, f32[512,4,2,256]{3,2,1,0:T(2,128)} %reshape.174, f32[256]{0:T(256)S(1)} %bitcast.124, f32[512,4,2]{0,2,1:T(2,128)S(1)} %rsqrt.30, bf16[512,4,256]{2,0,1:T(8,128)(2,1)S(1)} %bitcast.114, ...), kind=kOutput, calls=%fused_computation.3 | convolution fusion | flops 3252678656 | bytes 33326080 | tf_op jit(solution)/shard_map/tkgd,skd->kgts/dot_general | solution.py:146
  706.0 10.5 %fusion.12 = bf16[512,4,2,256]{0,3,2,1:T(8,128)(2,1)S(1)} fusion(bf16[1536,4,256,1]{0,2,3,1:T(8,128)(2,1)S(1)} %bitcast.112, f32[4,1536,512,2]{2,1,3,0:T(8,128)} %get-tuple-element.10, pred[512,1536]{0,1:T(8,128)(4,1)} %fusion.22, f32[512,4,2]{0,2,1:T(2,128)S(1)} %bitcast.125), kind=kOutput, calls=%fused_computation.22 | convolution fusion | flops 3242196992 | bytes 31211520 | tf_op jit(solution)/shard_map/kgts,skd->tkgd/dot_general | solution.py:152
  716.5 2.4 copy.72
  (63 shorter events, 26.6 us)
Async XLA Ops:
  6.5 83.7 %copy-start = (bf16[4,2560,48]{1,2,0:T(8,128)(2,1)S(1)}, bf16[4,2560,48]{1,2,0:T(8,128)(2,1)}, u32[]{:S(2)}) copy-start(bf16[4,2560,48]{1,2,0:T(8,128)(2,1)} %param.12) | copy-start | bytes 2949124
  90.3 1.5 copy-start.8
  106.0 126.0 %all-to-all-start.2 = ((bf16[16,4,16,4096]{3,2,1,0:T(8,128)(2,1)}), bf16[16,4,16,4096]{3,2,1,0:T(8,128)(2,1)}, u32[]{:S(2)}, u32[]{:S(2)}) async-start(bf16[16,4,16,4096]{3,2,1,0:T(8,128)(2,1)} %copy.62), calls=%async_computation.2 | async-start | bytes 16777216 | tf_op jit(solution)/shard_map/all_to_all | solution.py:105
  110.9 28.1 %all-gather.2.cloned.1.call-start = ((), (), s32[]{:S(2)}) async-start(), calls=%async_computation.3 | async-start | bytes 1474560 | tf_op jit(solution)/shard_map/all_gather | solution.py:80
  240.3 5.5 copy-start.10
  240.3 12.4 %copy-start.11 = (f32[2,256]{1,0:T(2,128)S(1)}, f32[2,256]{1,0:T(2,128)}, u32[]{:S(2)}) copy-start(f32[2,256]{1,0:T(2,128)} %param.11) | copy-start | bytes 6148
  240.3 324.3 %all-to-all-start = ((bf16[16,160,4096]{2,1,0:T(8,128)(2,1)}), bf16[16,160,4096]{2,1,0:T(8,128)(2,1)}, u32[]{:S(2)}, u32[]{:S(2)}) async-start(bf16[16,160,4096]{2,1,0:T(8,128)(2,1)} %stack.2), calls=%async_computation | async-start | bytes 41943040 | tf_op jit(solution)/shard_map/all_to_all | solution.py:12
  245.8 305.7 %collective-permute-start.2 = (s32[512]{0:T(512)S(1)}, s32[512]{0:T(512)S(1)}, u32[]{:S(2)}, u32[]{:S(2)}) collective-permute-start(s32[512]{0:T(512)S(1)} %copy-done.10), channel_id=1, source_target_pairs={{0,2},{1,3},{2,4},{3,5},{4,6},{5,7},{6,8},{7,9},{8,10},{9,11},{10,... | collective-permute-start | bytes 6152 | tf_op jit(solution)/shard_map/ppermute | solution.py:19
  250.4 301.1 %collective-permute-start.3 = (s32[512]{0:T(512)S(1)}, s32[512]{0:T(512)S(1)}, u32[]{:S(2)}, u32[]{:S(2)}) collective-permute-start(s32[512]{0:T(512)S(1)} %copy-done.10), channel_id=1, source_target_pairs={{0,1},{1,2},{2,3},{3,4},{4,5},{5,6},{6,7},{7,8},{8,9},{9,10},{10,1... | collective-permute-start | bytes 6152 | tf_op jit(solution)/shard_map/ppermute | solution.py:19
  551.5 13.1 %copy-start.9 = (f32[2560]{0:T(1024)S(1)}, f32[2560]{0:T(1024)}, u32[]{:S(2)}) copy-start(f32[2560]{0:T(1024)} %param.9) | copy-start | bytes 30724
  581.5 3.2 copy-start.2
  589.7 7.7 %copy-start.3 = (f32[512,4096]{1,0:T(8,128)S(1)}, f32[512,4096]{1,0:T(8,128)}, u32[]{:S(2)}) copy-start(f32[512,4096]{1,0:T(8,128)} %copy-done.2) | copy-start | bytes 25165828
  592.4 62.3 %collective-permute-start.5 = (bf16[512,1024]{1,0:T(8,128)(2,1)S(1)}, bf16[512,1024]{1,0:T(8,128)(2,1)}, u32[]{:S(2)}, u32[]{:S(2)}) collective-permute-start(bf16[512,1024]{1,0:T(8,128)(2,1)S(1)} %multiply_convert_fusion), channel_id=1, source_target_pairs={{0,1},{1,2},{2,3},{3,4},{4,5},{5,6},{6,7},{7,8},{8,9},{9,10},{10,1... | collective-permute-start | bytes 3145736 | tf_op jit(solution)/shard_map/ppermute | solution.py:19
  594.5 67.1 %collective-permute-start.4 = (bf16[512,1024]{1,0:T(8,128)(2,1)S(1)}, bf16[512,1024]{1,0:T(8,128)(2,1)}, u32[]{:S(2)}, u32[]{:S(2)}) collective-permute-start(bf16[512,1024]{1,0:T(8,128)(2,1)S(1)} %multiply_convert_fusion), channel_id=1, source_target_pairs={{0,2},{1,3},{2,4},{3,5},{4,6},{5,7},{6,8},{7,9},{8,10},{9,11},{10,... | collective-permute-start | bytes 3145736 | tf_op jit(solution)/shard_map/ppermute | solution.py:19
  597.5 75.3 %collective-permute-start = (bf16[512,1024]{1,0:T(8,128)(2,1)S(1)}, bf16[512,1024]{1,0:T(8,128)(2,1)}, u32[]{:S(2)}, u32[]{:S(2)}) collective-permute-start(bf16[512,1024]{1,0:T(8,128)(2,1)S(1)} %slice.85), channel_id=1, source_target_pairs={{0,2},{1,3},{2,4},{3,5},{4,6},{5,7},{6,8},{7,9},{8,10},{9,11},{10,... | collective-permute-start | bytes 3145736 | tf_op jit(solution)/shard_map/ppermute | solution.py:19
  600.4 83.7 %collective-permute-start.1 = (bf16[512,1024]{1,0:T(8,128)(2,1)S(1)}, bf16[512,1024]{1,0:T(8,128)(2,1)}, u32[]{:S(2)}, u32[]{:S(2)}) collective-permute-start(bf16[512,1024]{1,0:T(8,128)(2,1)S(1)} %slice.85), channel_id=1, source_target_pairs={{0,1},{1,2},{2,3},{3,4},{4,5},{5,6},{6,7},{7,8},{8,9},{9,10},{10,1... | collective-permute-start | bytes 3145736 | tf_op jit(solution)/shard_map/ppermute | solution.py:19
  687.1 4.9 copy-start.5
  687.1 4.9 copy-start.6
  687.1 4.9 copy-start.7
  692.0 13.9 %copy-start.4 = (bf16[1536,1024]{0,1:T(8,128)(2,1)S(1)}, bf16[1536,1024]{0,1:T(8,128)(2,1)}, u32[]{:S(2)}) copy-start(bf16[1536,1024]{0,1:T(8,128)(2,1)} %copy.80) | copy-start | bytes 9437188
  705.9 12.9 %copy-start.1 = (bf16[4,2560,48]{1,2,0:T(8,128)(2,1)S(1)}, bf16[4,2560,48]{1,2,0:T(8,128)(2,1)}, u32[]{:S(2)}) copy-start(bf16[4,2560,48]{1,2,0:T(8,128)(2,1)} %param.12) | copy-start | bytes 2949124
Sparse Core Ops, SparseCore 0:
  113.4 25.4 all-gather.1
